TPU v7x, 256 devices: a whole 4x4x8 slice. The times are simulated.
256 devices in a mesh: row: 16 (over y, x), col: 16 (over z, core).
Axes of the slice: x: 4, y: 4, z: 8, core: 2. Of those that a mesh axis runs over, the one named last changes fastest.
Arguments:
- unfolding: float32 [1024, 32768], P('row', 'col'), may hold values from -40 to 40, as said below
- factor: float32 [1024, 64], replicated, may hold values from -6 to 6
Outputs:
- gram_lower: float32 [1024, 1024], P(('row', 'col'))
- new_factor: float32 [1024, 64], replicated
- core: float32 [64, 32768], P('row', 'col')
Inputs may be any that keep to these rules, and one draw needn't show every extreme that they name: Entries of the unfolding are real values.
All inputs are finite; a program needn't handle non-finite values.
Results may differ from a plain program's by a relative error of at most 0.0003.
Values sent between devices are 32-bit elements; how exact they have to be, the bound alone decides.
A program may use at most 64 MiB of HBM per device.

v0:
```python
import math

import jax
import jax.numpy as jnp
from jax import lax
from jax.sharding import PartitionSpec as P


def orthonormal(image, mode):
    highest = lax.Precision.HIGHEST
    inner = jnp.dot(image.T, image, precision=highest, preferred_element_type=jnp.float32) / mode
    chol = jnp.linalg.cholesky(inner)
    return jax.scipy.linalg.solve_triangular(chol, image.T, lower=True).T


def body(unfolding, factor):
    highest = lax.Precision.HIGHEST
    n_row = lax.axis_size("row")
    n_col = lax.axis_size("col")
    devices = n_row * n_col
    regrouped = lax.all_to_all(unfolding, "row", split_axis=1, concat_axis=0, tiled=True)
    mode = regrouped.shape[0]
    total_cols = regrouped.shape[1] * devices
    half = mode // (2 * devices)
    partial_value = (
        lax.dot_general(
            regrouped,
            regrouped,
            (((1,), (1,)), ((), ())),
            precision=highest,
            preferred_element_type=jnp.float32,
        )
        / total_cols
    )
    blocks = partial_value.reshape(2 * devices, half, mode)
    first_half = blocks[:devices]
    second_half = blocks[devices:][::-1]
    owner = lax.axis_index(("row", "col"))
    local_rows = lax.broadcasted_iota(jnp.int32, (2 * half, mode), 0)
    local_cols = lax.broadcasted_iota(jnp.int32, (2 * half, mode), 1)
    source = jnp.where(
        local_rows < half,
        owner * half + local_rows,
        (2 * devices - 1 - owner) * half + local_rows - half,
    )
    stacked = jnp.concatenate([first_half, second_half], axis=1).reshape(2 * devices * half, mode)
    mine = lax.psum_scatter(stacked, ("row", "col"), scatter_dimension=0, tiled=True)
    gram_lower = jnp.where(local_cols <= source, mine, jnp.float32(0.0))
    projected = lax.dot_general(
        regrouped,
        factor,
        (((0,), (0,)), ((), ())),
        precision=highest,
        preferred_element_type=jnp.float32,
    )
    term = (
        jnp.dot(regrouped, projected, precision=highest, preferred_element_type=jnp.float32)
        / total_cols
    )
    image = lax.psum(term, ("row", "col"))
    new_factor = orthonormal(image, mode)
    scale = 1.0 / math.sqrt(mode)
    rows_here = unfolding.shape[0]
    factor_here = lax.dynamic_slice_in_dim(
        new_factor, lax.axis_index("row") * rows_here, rows_here, 0
    )
    core = lax.psum_scatter(
        lax.dot_general(
            factor_here,
            unfolding,
            (((0,), (0,)), ((), ())),
            precision=highest,
            preferred_element_type=jnp.float32,
        )
        * scale,
        "row",
        scatter_dimension=0,
        tiled=True,
    )
    return (gram_lower, new_factor, core)


def solution(mesh):
    in_specs = (P("row", "col"), P())
    out_specs = (P(("row", "col"), None), P(), P("row", "col"))
    return jax.shard_map(body, mesh=mesh, in_specs=in_specs, out_specs=out_specs, check_vma=False)
```

profile of v0, /device:TPU:1, one launch (start us, length us, event | category | flops | bytes accessed | tf_op | source)
XLA Modules:
  0.0 442.4 jit_solution(5091193176912430611)
XLA Ops:
  7.2 0.0 copy-start
  7.2 0.0 all-reduce.8.cloned.1.call-start
  7.2 1.0 copy-done
  8.3 17.8 %all_to_all.19 = f32[64,16,128]{2,0,1:T(8,128)S(1)} all-to-all(f32[64,16,128]{2,0,1:T(8,128)S(1)} %copy_bitcast_fusion), channel_id=1, replica_groups=mesh['row'=16,'col'=16] {'row'}, dimensions={1} | all-to-all | bytes 1048576 | tf_op jit(solution)/shard_map/all_to_all | solution.py:21
  26.1 3.4 convolution_multiply_fusion.1
  29.5 2.3 fusion.7
  31.7 2.5 slice.27
  34.2 2.0 rev.3
  36.3 0.0 copy-start.1
  36.3 3.6 slice.25
  39.9 0.0 copy-done.1
  39.9 5.4 %pad_maximum_fusion = f32[256,4,1024]{2,1,0:T(4,128)} fusion(f32[256,2,1024]{2,1,0:T(2,128)S(1)} %copy-done.1, f32[256,2,1024]{2,1,0:T(2,128)} %slice.25), kind=kLoop, calls=%fused_computation | loop fusion | flops 1048576 | bytes 8388608 | tf_op jit(solution)/shard_map/concatenate | solution.py:46
  45.3 0.0 copy-start.3
  45.3 5.3 %reshape.25 = f32[1024,1024]{1,0:T(8,128)} reshape(f32[256,4,1024]{2,1,0:T(4,128)} %pad_maximum_fusion) | data formatting | bytes 8388608 | tf_op jit(solution)/shard_map/reshape | solution.py:46
  50.7 0.0 copy-done.3
  50.7 0.4 fusion.8
  51.1 0.0 copy-start.4
  51.1 1.4 fusion
  52.5 0.0 all-reduce.8.cloned.1.call-update
  52.5 0.2 all-reduce.6.cloned.1.call-start
  52.8 270.4 %all-reduce.8.cloned.1.call-done = (f32[1024,1024]{1,0:T(8,128)}, f32[1024,64]{0,1:T(8,128)}) async-done(((f32[1024,1024]{1,0:T(8,128)}, f32[1024,64]{0,1:T(8,128)}), (f32[1024,1024]{1,0:T(8,128)}, f32[1024,64]{0,1:T(8,128)})) %all-reduce.8.cloned.1.call-update) | async-done | bytes 4456464
  323.2 1.4 fusion.9
  324.6 0.1 copy.10
  324.7 5.8 %cholesky.16 = f32[64,64]{1,0:T(8,128)S(1)} custom-call(f32[64,64]{1,0:T(8,128)S(1)} %fusion.4), custom_call_target="Cholesky" | custom-call | tf_op jit(solution)/shard_map/jit(cholesky)/cholesky | solution.py:12
  330.6 0.6 compare_reduce_fusion
  331.2 0.7 fusion.1
  331.9 4.9 %custom-call.7 = f32[1,64,64]{1,2,0:T(8,128)S(1)} custom-call(f32[1,64,64]{2,1,0:T(8,128)S(1)} %fusion.1), custom_call_target="InvertDiagBlocksLowerTriangular" | custom-call | tf_op jit(solution)/shard_map/jit(_solve_triangular)/triangular_solve | solution.py:13
  336.8 1.4 fusion.2
  338.2 0.0 copy-start.2
  338.2 1.5 convolution_multiply_fusion
  339.6 0.0 all-reduce.6.cloned.1.call-update
  339.7 0.0 copy-done.4
  339.7 0.6 dynamic-slice.1
  340.9 1.4 dynamic-slice_select_fusion
  342.4 91.7 %all-reduce.6.cloned.1.call-done = f32[64,2048]{1,0:T(8,128)} async-done(((f32[64,2048]{1,0:T(8,128)}), f32[64,2048]{1,0:T(8,128)}) %all-reduce.6.cloned.1.call-update) | async-done | bytes 524304
  434.1 1.5 constant_dynamic-slice_fusion
  435.5 0.0 copy-done.2
  (5 shorter events, 0.1 us)
Async XLA Ops:
  7.2 1.0 copy-start
  7.2 316.0 %all-reduce.8.cloned.1.call-start = ((), (), s32[]{:S(2)}) async-start(), calls=%async_computation.2 | async-start | bytes 8912896
  36.3 3.6 copy-start.1
  45.3 5.4 %copy-start.3 = (f32[1024,64]{0,1:T(8,128)S(1)}, f32[1024,64]{0,1:T(8,128)}, u32[]{:S(2)}) copy-start(f32[1024,64]{0,1:T(8,128)} %param.3) | copy-start | bytes 786436
  51.1 288.6 %copy-start.4 = (u32[256]{0:T(256)S(1)}, u32[256]{0:T(256)}, u32[]{:S(2)}) copy-start(u32[256]{0:T(256)} %constant.81) | copy-start | bytes 3076
  52.5 381.5 %all-reduce.6.cloned.1.call-start = ((), (), s32[]{:S(2)}) async-start(), calls=%async_computation.1 | async-start | bytes 1048576
  338.2 97.4 %copy-start.2 = (f32[1024,64]{0,1:T(8,128)}, f32[1024,64]{0,1:T(8,128)S(1)}, u32[]{:S(2)}) copy-start(f32[1024,64]{0,1:T(8,128)S(1)} %fusion.2) | copy-start | bytes 786436
Sparse Core Ops, SparseCore 0:
  52.7 270.5 all-reduce.7
  339.8 94.2 all-reduce.5
where the time goes:
time: 444 us; the launch traced here: 442 us
  waiting for transfers between devices  362 us (82%)
  other arithmetic  19 us (4%)
  local copies, waits for them, and re-layouts  18.9 us (4%)
  blocking collectives  17.8 us (4%)
  between operations  14.8 us (3%)
  matrix products  9.47 us (2%)
    unnamed x4, waiting for transfers between devices  362 us
    all_to_all x1, blocking collectives, body(): lax.all_to_all(unfolding, 'row', split_axis=1, concat_axis=0, tiled=True)  17.8 us
  transfers between devices with their start and end apart: 2, of which 2 were waited for; matrix products, arithmetic and copies ran while one was open for 0% of the time, Pallas kernels for 0%

commit v1 on v0

v1 whole, which is shorter than its diff:
```python
import functools
import math

import jax
import jax.numpy as jnp
from jax import lax
from jax.experimental import pallas as pl
from jax.experimental.pallas import tpu as pltpu
from jax.sharding import PartitionSpec as P

F32 = jnp.float32
BF16 = jnp.bfloat16
HIGHEST = lax.Precision.HIGHEST
MESH = pl.DeviceIdType.MESH

NY, NX, NZ, NK = 4, 4, 8, 2
NR = NY * NX
MODE, RANK, COLS = 1024, 64, 32768
ROWS = MODE // NR
LANES = 128
GW = 1152

PLANE = [(oy, ox) for oy in range(NY) for ox in range(NX) if (oy, ox) != (0, 0)]
PLANE.sort(key=lambda o: -(min(o[0], NY - o[0]) + min(o[1], NX - o[1])))
PLANE_K = [(oy, ox, ok) for oy in range(NY) for ox in range(NX) for ok in range(NK)]
PLANE_K = [o for o in PLANE_K if o != (0, 0, 0)]
PLANE_K.sort(key=lambda o: -(min(o[0], NY - o[0]) + min(o[1], NX - o[1])))
ZS = sorted(range(1, NZ), key=lambda o: -min(o, NZ - o))


def dot_t(a, b, precision=None):
    return lax.dot_general(
        a, b, (((1,), (1,)), ((), ())), precision=precision, preferred_element_type=F32
    )


def dot(a, b, precision=None):
    return lax.dot_general(
        a, b, (((1,), (0,)), ((), ())), precision=precision, preferred_element_type=F32
    )


def eliminate(inner):
    lane = lax.broadcasted_iota(jnp.int32, (8, 128), 1)
    sub = lax.broadcasted_iota(jnp.int32, (8, 128), 0)
    tiles = []
    for v in range(RANK // 8):
        unit = jnp.where(lane == sub + (8 * v + RANK), F32(1.0), F32(0.0))
        tiles.append(jnp.where(lane < RANK, inner[8 * v : 8 * v + 8, :], unit))
    scales = [jnp.zeros((8, 128), F32) for _ in tiles]
    for j in range(RANK):
        vj, sj = j // 8, j % 8
        cols = {
            v: jnp.broadcast_to(tiles[v][:, j : j + 1], (8, 128)) for v in range(vj, RANK // 8)
        }
        row = jnp.broadcast_to(tiles[vj][sj : sj + 1, :], (8, 128))
        pivot = jnp.broadcast_to(cols[vj][sj : sj + 1, :], (8, 128))
        scales[vj] = jnp.where(sub == sj, pivot, scales[vj])
        row = row * (1.0 / pivot)
        for v in range(vj, RANK // 8):
            update = cols[v] * row
            if v == vj:
                update = jnp.where(sub > sj, update, 0.0)
            tiles[v] = tiles[v] - update
    out = [jnp.where(lane < RANK, 0.0, t * (1.0 / jnp.sqrt(s))) for t, s in zip(tiles, scales)]
    return jnp.concatenate(out, axis=0)


def kernel(
    x_hbm,
    f_ref,
    gram_out,
    nf_out,
    core_out,
    xr,
    ft,
    xcat,
    img_send,
    img_recv,
    z_send,
    z_recv,
    p_send,
    p_all,
    c_send,
    c_recv,
    lhs,
    rhs,
    g_send,
    g_recv,
    gz_send,
    gz_recv,
    gfin,
    own_sem,
    x_ss,
    x_rs,
    pair_ss,
    pair_rs,
    img_ss,
    img_rs,
    z_ss,
    z_rs,
    p_ss,
    p_rs,
    c_ss,
    c_rs,
    g_ss,
    g_rs,
    gz_ss,
    gz_rs,
):
    r = lax.axis_index("row")
    c = lax.axis_index("col")
    y, x = r // NX, r % NX
    z, k = c // NK, c % NK

    def plane(oy, ox):
        return ((y + oy) % NY) * NX + (x + ox) % NX

    def column(zz, kk):
        return zz * NK + kk

    def send(src, dst, ss, rs, row, col):
        copy = pltpu.make_async_remote_copy(
            src_ref=src,
            dst_ref=dst,
            send_sem=ss,
            recv_sem=rs,
            device_id=(row, col),
            device_id_type=MESH,
        )
        copy.start()
        return copy

    def arrival(dst, ss, rs):
        return pltpu.make_async_remote_copy(
            src_ref=dst,
            dst_ref=dst,
            send_sem=ss,
            recv_sem=rs,
            device_id=(r, c),
            device_id_type=MESH,
        )

    barrier = pltpu.get_barrier_semaphore()
    peers = 0
    for oy, ox, ok in PLANE_K:
        pl.semaphore_signal(
            barrier,
            inc=1,
            device_id=(plane(oy, ox), column(z, (k + ok) % NK)),
            device_id_type=MESH,
        )
        peers += 1
    for oz in ZS:
        for ok in range(NK):
            pl.semaphore_signal(
                barrier,
                inc=1,
                device_id=(r, column((z + oz) % NZ, (k + ok) % NK)),
                device_id_type=MESH,
            )
            peers += 1
    pl.semaphore_wait(barrier, peers)

    pending = []

    def columns_of(row):
        return pl.ds(pl.multiple_of(row * LANES, LANES), LANES)

    for i, (oy, ox) in enumerate(PLANE):
        to = plane(oy, ox)
        pending.append(
            send(x_hbm.at[:, columns_of(to)], xr.at[0, r], x_ss.at[i], x_rs.at[r], to, c)
        )
    own = pltpu.make_async_copy(x_hbm.at[:, columns_of(r)], xr.at[0, r], own_sem)
    own.start()
    ft[...] = f_ref[...].T
    own.wait()
    for oy, ox in PLANE:
        frm = plane(oy, ox)
        arrival(xr.at[0, frm], x_ss.at[0], x_rs.at[frm]).wait_recv()
    partner = column(z, 1 - k)
    pending.append(send(xr.at[0], xr.at[1], pair_ss, pair_rs, r, partner))

    rows = xr[0]
    flat = rows.reshape(MODE, LANES)
    xcat[:, 0:LANES] = rows[:, 0 : ROWS // 2, :].reshape(MODE // 2, LANES)
    xcat[:, LANES : 2 * LANES] = rows[:, ROWS // 2 :, :].reshape(MODE // 2, LANES)
    yt = dot(ft[...], flat, HIGHEST) * F32(1.0 / COLS)
    zero = jnp.zeros_like(yt)
    weights = jnp.concatenate(
        [jnp.concatenate([yt, zero], axis=1), jnp.concatenate([zero, yt], axis=1)], axis=0
    )
    term = dot_t(xcat[...], weights, HIGHEST)
    img_send[...] = term.reshape(NR, NK, 16, 128)
    me = r * NK + k
    for i, (oy, ox, ok) in enumerate(PLANE_K):
        to, kk = plane(oy, ox), (k + ok) % NK
        pending.append(
            send(
                img_send.at[to, kk],
                img_recv.at[me],
                img_ss.at[i],
                img_rs.at[me],
                to,
                column(z, kk),
            )
        )
    img_recv[me] = img_send[r, k]

    arrival(xr.at[1], pair_ss, pair_rs).wait_recv()
    for s in range(2):
        whole = xr[s].reshape(MODE, LANES)
        hi = whole.astype(BF16)
        lo = (whole - hi.astype(F32)).astype(BF16)
        rhs[:, s * LANES : (s + 1) * LANES] = hi
        rhs[:, (2 + s) * LANES : (3 + s) * LANES] = lo
        rhs[:, (4 + s) * LANES : (5 + s) * LANES] = hi
    for b in range(2 * NR):
        half = k if b < NR else 1 - k
        at = pl.ds(pl.multiple_of(32 * b + 16 * half, 16), 16)
        lhs[16 * b : 16 * b + 16, 0:256] = rhs[at, 0:256]
        lhs[16 * b : 16 * b + 16, 256:512] = rhs[at, 0:256]
        lhs[16 * b : 16 * b + 16, 512:768] = rhs[at, 256:512]
    for nb in range(4):
        part = dot_t(lhs[128 * nb : 512, :], rhs[256 * nb : 256 * nb + 256, :]) * F32(1.0 / COLS)
        for b in range(8 * nb, 2 * NR):
            to = b if b < NR else 2 * NR - 1 - b
            off = 0 if b < NR else 128 * (8 - b // 4)
            width = min(256, 128 * (b // 4 + 1) - 256 * nb)
            rows_b = part[16 * (b - 8 * nb) : 16 * (b - 8 * nb) + 16, 0:width]
            g_send[to, :, off + 256 * nb : off + 256 * nb + width] = rows_b

    for oy, ox, ok in PLANE_K:
        frm = plane(oy, ox) * NK + (k + ok) % NK
        arrival(img_recv.at[frm], img_ss.at[0], img_rs.at[frm]).wait_recv()
    total = img_recv[0]
    for s in range(1, NR * NK):
        total = total + img_recv[s]
    z_send[...] = total
    z_recv[z] = total
    for i, oz in enumerate(ZS):
        pending.append(
            send(z_send, z_recv.at[z], z_ss.at[i], z_rs.at[z], r, column((z + oz) % NZ, k))
        )
    for oz in ZS:
        frm = (z + oz) % NZ
        arrival(z_recv.at[frm], z_ss.at[0], z_rs.at[frm]).wait_recv()
    total = z_recv[0]
    for s in range(1, NZ):
        total = total + z_recv[s]
    p_send[...] = total
    p_all[me] = total
    for i, (oy, ox, ok) in enumerate(PLANE_K):
        pending.append(
            send(
                p_send,
                p_all.at[me],
                p_ss.at[i],
                p_rs.at[me],
                plane(oy, ox),
                column(z, (k + ok) % NK),
            )
        )

    for i, (oy, ox) in enumerate(PLANE):
        to = plane(oy, ox)
        pending.append(send(g_send.at[to], g_recv.at[r], g_ss.at[i], g_rs.at[r], to, c))
    g_recv[r] = g_send[r]

    for oy, ox, ok in PLANE_K:
        frm = plane(oy, ox) * NK + (k + ok) % NK
        arrival(p_all.at[frm], p_ss.at[0], p_rs.at[frm]).wait_recv()

    image = p_all[...].reshape(MODE // 2, 128)
    image_t = image.T
    inner2 = dot(image_t, image, HIGHEST)
    products = dot(image_t, xcat[...], HIGHEST)
    inner = (inner2[0:RANK, :] + pltpu.roll(inner2[RANK:, :], RANK, 1)) * F32(1.0 / MODE)
    product = products[0:RANK, 0:LANES] + products[RANK:, LANES:]
    inv_high = eliminate(inner)
    inv_low = pltpu.roll(inv_high, RANK, 1)
    core = dot(inv_low[:, 0:RANK], product, HIGHEST) * F32(1.0 / math.sqrt(MODE))
    c_send[...] = core.reshape(NR, RANK // NR, LANES)
    for i, (oy, ox) in enumerate(PLANE):
        to = plane(oy, ox)
        pending.append(send(c_send.at[to], c_recv.at[r], c_ss.at[i], c_rs.at[r], to, c))
    c_recv[r] = c_send[r]
    top = dot_t(image, inv_low, HIGHEST).reshape(NR, ROWS // 2, RANK)
    bottom = dot_t(image, inv_high, HIGHEST).reshape(NR, ROWS // 2, RANK)
    nf_out[...] = jnp.concatenate([top, bottom], axis=1).reshape(MODE, RANK)

    for oy, ox in PLANE:
        frm = plane(oy, ox)
        arrival(g_recv.at[frm], g_ss.at[0], g_rs.at[frm]).wait_recv()
    total = g_recv[0]
    for s in range(1, NR):
        total = total + g_recv[s]
    low_width = 128 * (r // 4 + 1)
    lane = lax.broadcasted_iota(jnp.int32, (2, GW), 1)
    for t in range(8):
        pair = jnp.where(lane < low_width, total[2 * t : 2 * t + 2], total[14 - 2 * t : 16 - 2 * t])
        gz_send[t] = pair
    for t in range(8):
        zz, kk = 4 * k + t // 2, t % 2
        mine = jnp.logical_and(zz == z, kk == k)

        @pl.when(jnp.logical_not(mine))
        def _():
            send(gz_send.at[t], gz_recv.at[z], gz_ss.at[t], gz_rs.at[z], r, column(zz, kk))

        @pl.when(mine)
        def _():
            gz_recv[z] = gz_send[t]

    for oy, ox in PLANE:
        frm = plane(oy, ox)
        arrival(c_recv.at[frm], c_ss.at[0], c_rs.at[frm]).wait_recv()
    for s in range(NR):
        core_out[:, LANES * s : LANES * (s + 1)] = c_recv[s]

    from_core = z // 4
    for s in range(NZ):

        @pl.when(jnp.logical_not(jnp.logical_and(s == z, from_core == k)))
        def _():
            arrival(gz_recv.at[s], gz_ss.at[0], gz_rs.at[s]).wait_recv()

    total = gz_recv[0]
    for s in range(1, NZ):
        total = total + gz_recv[s]
    gfin[...] = jnp.zeros_like(gfin)
    gfin[:, 0:GW] = total
    owner = r * (NZ * NK) + c
    row_id = lax.broadcasted_iota(jnp.int32, (2, MODE), 0)
    col_id = lax.broadcasted_iota(jnp.int32, (2, MODE), 1)
    low = gfin[:, 0:MODE]
    high = gfin[:, pl.ds(pl.multiple_of(low_width, 128), MODE)]
    gram_out[0:2, :] = jnp.where(col_id <= 2 * owner + row_id, low, 0.0)
    gram_out[2:4, :] = jnp.where(col_id <= MODE - 2 - 2 * owner + row_id, high, 0.0)

    for copy in pending:
        copy.wait_send()
    for t in range(8):
        zz, kk = 4 * k + t // 2, t % 2

        @pl.when(jnp.logical_not(jnp.logical_and(zz == z, kk == k)))
        def _():
            arrival(gz_send.at[t], gz_ss.at[t], gz_rs.at[0]).wait_send()


def body(unfolding, factor):
    dma = pltpu.SemaphoreType.DMA
    vmem = pl.BlockSpec(memory_space=pltpu.VMEM)
    return pl.pallas_call(
        kernel,
        out_shape=(
            jax.ShapeDtypeStruct((4, MODE), F32),
            jax.ShapeDtypeStruct((MODE, RANK), F32),
            jax.ShapeDtypeStruct((RANK // NR, LANES * NR), F32),
        ),
        in_specs=[pl.BlockSpec(memory_space=pl.ANY), vmem],
        out_specs=(vmem, vmem, vmem),
        scratch_shapes=[
            pltpu.VMEM((2, NR, ROWS, LANES), F32),
            pltpu.VMEM((RANK, MODE), F32),
            pltpu.VMEM((MODE // 2, 2 * LANES), F32),
            pltpu.VMEM((NR, NK, 16, 128), F32),
            pltpu.VMEM((NR * NK, 16, 128), F32),
            pltpu.VMEM((16, 128), F32),
            pltpu.VMEM((NZ, 16, 128), F32),
            pltpu.VMEM((16, 128), F32),
            pltpu.VMEM((NR * NK, 16, 128), F32),
            pltpu.VMEM((NR, RANK // NR, LANES), F32),
            pltpu.VMEM((NR, RANK // NR, LANES), F32),
            pltpu.VMEM((MODE // 2, 6 * LANES), BF16),
            pltpu.VMEM((MODE, 6 * LANES), BF16),
            pltpu.VMEM((NR, 16, GW), F32),
            pltpu.VMEM((NR, 16, GW), F32),
            pltpu.VMEM((8, 2, GW), F32),
            pltpu.VMEM((NZ, 2, GW), F32),
            pltpu.VMEM((2, 1536), F32),
            dma,
            dma((NR - 1,)),
            dma((NR,)),
            dma,
            dma,
            dma((NR * NK - 1,)),
            dma((NR * NK,)),
            dma((NZ - 1,)),
            dma((NZ,)),
            dma((NR * NK - 1,)),
            dma((NR * NK,)),
            dma((NR - 1,)),
            dma((NR,)),
            dma((NR - 1,)),
            dma((NR,)),
            dma((8,)),
            dma((NZ,)),
        ],
        compiler_params=pltpu.CompilerParams(collective_id=0, has_side_effects=True),
        name="tucker_update",
    )(unfolding, factor)


def solution(mesh):
    in_specs = (P("row", "col"), P())
    out_specs = (P(("row", "col"), None), P(), P("row", "col"))
    return jax.shard_map(body, mesh=mesh, in_specs=in_specs, out_specs=out_specs, check_vma=False)
```

time: 444 us -> 69.7 us (0.16)
  waiting for transfers between devices: 362 us -> 0 us
  Pallas kernels: 0 us -> 63.5 us
  other arithmetic: 19 us -> 0 us
  blocking collectives: 17.8 us -> 0 us
  between operations: 14.8 us -> 0.65 us
  local copies, waits for them, and re-layouts: 18.9 us -> 5.27 us
  matrix products: 9.47 us -> 0 us
    unnamed x4 -> x0, waiting for transfers between devices: 362 us -> none
    pallas_call x0 -> x1, Pallas kernels: none -> 63.5 us  [body(): pl.pallas_call(kernel, out_shape=(jax.ShapeDtypeStruct((4, MODE), F32), j...]
    all_to_all x1 -> x0, blocking collectives: 17.8 us -> none  [body(): lax.all_to_all(unfolding, 'row', split_axis=1, concat_axis=0, tiled=True)]
    another operation x5 -> x0, other arithmetic: 12.1 us -> none  [the longest x3 6.52 us: orthonormal(): chol = jnp.linalg.cholesky(inner)]
    slice x3 -> x0, local copies, waits for them, and re-layouts: 8.36 us -> none  [the longest x2 5.87 us: body(): first_half = blocks[:devices]]
    dot_general x5 -> x0, matrix products: 8.09 us -> none  [the longest x1 3.42 us: body(): lax.dot_general(regrouped, regrouped, (((1,), (1,)), ((), ())), precision...]
    concatenate x1 -> x0, other arithmetic: 5.42 us -> none  [body(): jnp.concatenate([first_half, second_half], axis=1)]
    reshape x1 -> x0, local copies, waits for them, and re-layouts: 5.35 us -> none  [body(): jnp.concatenate([first_half, second_half], axis=1)]
  transfers between devices with their start and end apart: 2 -> 0, of which waited for: 2 -> 0; matrix products, arithmetic and copies ran while one was open for 0% -> 0% of each run, Pallas kernels for 0% -> 0%
where the time goes in v1:
time: 69.7 us; the launch traced here: 69.4 us
  Pallas kernels  63.5 us (91%)
  local copies, waits for them, and re-layouts  5.27 us (8%)
    pallas_call x1, Pallas kernels, body(): pl.pallas_call(kernel, out_shape=(jax.ShapeDtypeStruct((4, MODE), F32), j...  63.5 us
    unnamed x7, local copies, waits for them, and re-layouts  3.33 us
    pallas_call x1, local copies, waits for them, and re-layouts, body(): pl.pallas_call(kernel, out_shape=(jax.ShapeDtypeStruct((4, MODE), F32), j...  1.93 us

profile of v1, /device:TPU:1, one launch (start us, length us, event | category | flops | bytes accessed | tf_op | source)
XLA Modules:
  0.0 69.4 jit_solution(17280517752075951467)
XLA Ops:
  0.6 1.9 %copy.5.f_ref = f32[1024,64]{1,0:T(8,128)} copy(f32[1024,64]{0,1:T(8,128)} %param.3) | data formatting | bytes 524288 | tf_op args[1]
  2.6 63.5 %tucker_update.1 = (f32[4,1024]{1,0:T(4,128)}, f32[1024,64]{1,0:T(8,128)}, f32[4,2048]{1,0:T(4,128)}) custom-call(f32[64,2048]{1,0:T(8,128)} %x_hbm.1, f32[1024,64]{1,0:T(8,128)} %copy.5.f_ref), custom_call_target="tpu_custom_call" | custom-call | tf_op jit(solution)/shard_map/tucker_update/pallas_call | solution.py:355
  66.1 0.0 copy-start.1
  66.1 1.9 %copy.6 = f32[1024,64]{0,1:T(8,128)} copy(f32[1024,64]{1,0:T(8,128)} %get-tuple-element.4) | data formatting | bytes 524288 | tf_op jit(solution)/shard_map/tucker_update/pallas_call | solution.py:355
  68.0 0.0 copy-done.1
  68.0 0.0 copy-start
  68.0 0.6 copy.9
  68.6 0.2 copy-done
  68.8 0.6 copy.10
Async XLA Ops:
  66.1 1.9 %copy-start.1 = (f32[4,1024]{1,0:T(4,128)S(1)}, f32[4,1024]{1,0:T(4,128)}, u32[]{:S(2)}) copy-start(f32[4,1024]{1,0:T(4,128)} %get-tuple-element.9) | copy-start | bytes 49156
  68.0 0.8 %copy-start = (f32[4,2048]{1,0:T(4,128)S(1)}, f32[4,2048]{1,0:T(4,128)}, u32[]{:S(2)}) copy-start(f32[4,2048]{1,0:T(4,128)} %get-tuple-element.11) | copy-start | bytes 98308

commit v2 on v1

--- a/solution.py
+++ b/solution.py
@@ -68,12 +68,11 @@
 
 def kernel(
     x_hbm,
-    f_ref,
+    ft,
     gram_out,
     nf_out,
     core_out,
     xr,
-    ft,
     xcat,
     img_send,
     img_recv,
@@ -174,7 +173,6 @@
         )
     own = pltpu.make_async_copy(x_hbm.at[:, columns_of(r)], xr.at[0, r], own_sem)
     own.start()
-    ft[...] = f_ref[...].T
     own.wait()
     for oy, ox in PLANE:
         frm = plane(oy, ox)
@@ -182,10 +180,9 @@
     partner = column(z, 1 - k)
     pending.append(send(xr.at[0], xr.at[1], pair_ss, pair_rs, r, partner))
 
-    rows = xr[0]
-    flat = rows.reshape(MODE, LANES)
-    xcat[:, 0:LANES] = rows[:, 0 : ROWS // 2, :].reshape(MODE // 2, LANES)
-    xcat[:, LANES : 2 * LANES] = rows[:, ROWS // 2 :, :].reshape(MODE // 2, LANES)
+    flat = xr[0].reshape(MODE, LANES)
+    xcat[:, 0:LANES] = flat[0 : MODE // 2]
+    xcat[:, LANES : 2 * LANES] = flat[MODE // 2 :]
     yt = dot(ft[...], flat, HIGHEST) * F32(1.0 / COLS)
     zero = jnp.zeros_like(yt)
     weights = jnp.concatenate(
@@ -286,9 +283,8 @@
         to = plane(oy, ox)
         pending.append(send(c_send.at[to], c_recv.at[r], c_ss.at[i], c_rs.at[r], to, c))
     c_recv[r] = c_send[r]
-    top = dot_t(image, inv_low, HIGHEST).reshape(NR, ROWS // 2, RANK)
-    bottom = dot_t(image, inv_high, HIGHEST).reshape(NR, ROWS // 2, RANK)
-    nf_out[...] = jnp.concatenate([top, bottom], axis=1).reshape(MODE, RANK)
+    nf_out[:, 0 : MODE // 2] = dot_t(inv_low, image, HIGHEST)
+    nf_out[:, MODE // 2 :] = dot_t(inv_high, image, HIGHEST)
 
     for oy, ox in PLANE:
         frm = plane(oy, ox)
@@ -352,18 +348,17 @@
 def body(unfolding, factor):
     dma = pltpu.SemaphoreType.DMA
     vmem = pl.BlockSpec(memory_space=pltpu.VMEM)
-    return pl.pallas_call(
+    gram_lower, new_factor_t, core = pl.pallas_call(
         kernel,
         out_shape=(
             jax.ShapeDtypeStruct((4, MODE), F32),
-            jax.ShapeDtypeStruct((MODE, RANK), F32),
+            jax.ShapeDtypeStruct((RANK, MODE), F32),
             jax.ShapeDtypeStruct((RANK // NR, LANES * NR), F32),
         ),
         in_specs=[pl.BlockSpec(memory_space=pl.ANY), vmem],
         out_specs=(vmem, vmem, vmem),
         scratch_shapes=[
             pltpu.VMEM((2, NR, ROWS, LANES), F32),
-            pltpu.VMEM((RANK, MODE), F32),
             pltpu.VMEM((MODE // 2, 2 * LANES), F32),
             pltpu.VMEM((NR, NK, 16, 128), F32),
             pltpu.VMEM((NR * NK, 16, 128), F32),
@@ -400,7 +395,8 @@
         ],
         compiler_params=pltpu.CompilerParams(collective_id=0, has_side_effects=True),
         name="tucker_update",
-    )(unfolding, factor)
+    )(unfolding, factor.T)
+    return gram_lower, new_factor_t.T, core
 
 
 def solution(mesh):

time: 69.7 us -> 68.1 us (0.977)
  local copies, waits for them, and re-layouts: 5.27 us -> 3.62 us
    pallas_call x1 -> x0, local copies, waits for them, and re-layouts: 1.93 us -> none  [body(): pl.pallas_call(kernel, out_shape=(jax.ShapeDtypeStruct((4, MODE), F32), j...]
    unnamed x7 -> x5, local copies, waits for them, and re-layouts: 3.33 us -> 3.62 us
where the time goes in v2:
time: 68.1 us; the launch traced here: 67.9 us
  Pallas kernels  63.6 us (93%)
  local copies, waits for them, and re-layouts  3.62 us (5%)
    pallas_call x1, Pallas kernels, body(): pl.pallas_call(kernel, out_shape=(jax.ShapeDtypeStruct((4, MODE), F32), j...  63.6 us
    unnamed x5, local copies, waits for them, and re-layouts  3.62 us

profile of v2, /device:TPU:1, one launch (start us, length us, event | category | flops | bytes accessed | tf_op | source)
XLA Modules:
  0.0 67.9 jit_solution(15225796273639289923)
XLA Ops:
  0.6 63.6 %tucker_update.1 = (f32[4,1024]{1,0:T(4,128)}, f32[64,1024]{1,0:T(8,128)}, f32[4,2048]{1,0:T(4,128)}) custom-call(f32[64,2048]{1,0:T(8,128)} %x_hbm.1, f32[64,1024]{1,0:T(8,128)} %bitcast.2), custom_call_target="tpu_custom_call" | custom-call | tf_op jit(solution)/shard_map/tucker_update/pallas_call | solution.py:351
  64.3 1.3 %copy.8 = f32[4,1024]{1,0:T(4,128)} copy(f32[4,1024]{1,0:T(4,128)} %get-tuple-element.12) | data formatting | bytes 32768
  65.6 0.0 copy-start
  65.6 1.7 %copy.9 = f32[1024,64]{0,1:T(8,128)} copy(f32[1024,64]{0,1:T(8,128)} %bitcast.3) | data formatting | bytes 524288
  67.3 0.0 copy-done
  67.3 0.6 copy.10
Async XLA Ops:
  65.6 1.7 %copy-start = (f32[4,2048]{1,0:T(4,128)S(1)}, f32[4,2048]{1,0:T(4,128)}, u32[]{:S(2)}) copy-start(f32[4,2048]{1,0:T(4,128)} %get-tuple-element.14) | copy-start | bytes 98308

commit v3 on v2

--- a/solution.py
+++ b/solution.py
@@ -25,6 +25,7 @@
 PLANE_K = [(oy, ox, ok) for oy in range(NY) for ox in range(NX) for ok in range(NK)]
 PLANE_K = [o for o in PLANE_K if o != (0, 0, 0)]
 PLANE_K.sort(key=lambda o: -(min(o[0], NY - o[0]) + min(o[1], NX - o[1])))
+OFFSETS = (2, 1, 3)
 ZS = sorted(range(1, NZ), key=lambda o: -min(o, NZ - o))
 
 
@@ -47,23 +48,38 @@
     for v in range(RANK // 8):
         unit = jnp.where(lane == sub + (8 * v + RANK), F32(1.0), F32(0.0))
         tiles.append(jnp.where(lane < RANK, inner[8 * v : 8 * v + 8, :], unit))
-    scales = [jnp.zeros((8, 128), F32) for _ in tiles]
-    for j in range(RANK):
-        vj, sj = j // 8, j % 8
-        cols = {
-            v: jnp.broadcast_to(tiles[v][:, j : j + 1], (8, 128)) for v in range(vj, RANK // 8)
-        }
-        row = jnp.broadcast_to(tiles[vj][sj : sj + 1, :], (8, 128))
-        pivot = jnp.broadcast_to(cols[vj][sj : sj + 1, :], (8, 128))
-        scales[vj] = jnp.where(sub == sj, pivot, scales[vj])
-        row = row * (1.0 / pivot)
-        for v in range(vj, RANK // 8):
-            update = cols[v] * row
-            if v == vj:
-                update = jnp.where(sub > sj, update, 0.0)
-            tiles[v] = tiles[v] - update
-    out = [jnp.where(lane < RANK, 0.0, t * (1.0 / jnp.sqrt(s))) for t, s in zip(tiles, scales)]
-    return jnp.concatenate(out, axis=0)
+
+    def over_lanes(tile, j):
+        return jnp.broadcast_to(tile[:, j : j + 1], (8, 128))
+
+    def over_rows(tile, i):
+        return jnp.broadcast_to(tile[i : i + 1, :], (8, 128))
+
+    for v in range(RANK // 8):
+        panel = tiles[v]
+        spread = [over_lanes(panel, 8 * v + j) for j in range(8)]
+        scale = jnp.ones((8, 128), F32)
+        rows, links = [], []
+        for s in range(8):
+            pivot = over_rows(spread[s], s)
+            inverse = 1.0 / pivot
+            scale = jnp.where(sub == s, pivot, scale)
+            row = over_rows(panel, s) * inverse
+            link = [over_rows(spread[j], s) * inverse for j in range(s + 1, 8)]
+            factor = jnp.where(sub > s, spread[s], 0.0)
+            for j in range(s + 1, 8):
+                spread[j] = spread[j] - factor * link[j - s - 1]
+            panel = panel - factor * row
+            rows.append(row)
+            links.append(link)
+        tiles[v] = panel * (1.0 / jnp.sqrt(scale))
+        for w in range(v + 1, RANK // 8):
+            spread = [over_lanes(tiles[w], 8 * v + j) for j in range(8)]
+            for s in range(8):
+                for j in range(s + 1, 8):
+                    spread[j] = spread[j] - spread[s] * links[s][j - s - 1]
+                tiles[w] = tiles[w] - spread[s] * rows[s]
+    return jnp.concatenate([jnp.where(lane < RANK, 0.0, t) for t in tiles], axis=0)
 
 
 def kernel(
@@ -84,8 +100,10 @@
     c_recv,
     lhs,
     rhs,
-    g_send,
-    g_recv,
+    ga,
+    ga_recv,
+    gb,
+    gb_recv,
     gz_send,
     gz_recv,
     gfin,
@@ -102,8 +120,10 @@
     p_rs,
     c_ss,
     c_rs,
-    g_ss,
-    g_rs,
+    ga_ss,
+    ga_rs,
+    gb_ss,
+    gb_rs,
     gz_ss,
     gz_rs,
 ):
@@ -226,7 +246,17 @@
             off = 0 if b < NR else 128 * (8 - b // 4)
             width = min(256, 128 * (b // 4 + 1) - 256 * nb)
             rows_b = part[16 * (b - 8 * nb) : 16 * (b - 8 * nb) + 16, 0:width]
-            g_send[to, :, off + 256 * nb : off + 256 * nb + width] = rows_b
+            at = pl.ds(off + 256 * nb, width)
+            ga[0, to % NX, to // NX, :, at] = rows_b[0:8]
+            ga[1, to // NX, to % NX, :, at] = rows_b[8:16]
+    for i in range(3):
+        xx, yy = (x + OFFSETS[i]) % NX, (y + OFFSETS[i]) % NY
+        pending.append(
+            send(ga.at[0, xx], ga_recv.at[0, x], ga_ss.at[0, i], ga_rs.at[0, x], y * NX + xx, c)
+        )
+        pending.append(
+            send(ga.at[1, yy], ga_recv.at[1, y], ga_ss.at[1, i], ga_rs.at[1, y], yy * NX + x, c)
+        )
 
     for oy, ox, ok in PLANE_K:
         frm = plane(oy, ox) * NK + (k + ok) % NK
@@ -260,10 +290,21 @@
             )
         )
 
-    for i, (oy, ox) in enumerate(PLANE):
-        to = plane(oy, ox)
-        pending.append(send(g_send.at[to], g_recv.at[r], g_ss.at[i], g_rs.at[r], to, c))
-    g_recv[r] = g_send[r]
+    for h, at in ((0, x), (1, y)):
+        total = ga[h, at]
+        for i in range(3):
+            frm = (at + OFFSETS[i]) % 4
+            arrival(ga_recv.at[h, frm], ga_ss.at[h, 0], ga_rs.at[h, frm]).wait_recv()
+            total = total + ga_recv[h, frm]
+        gb[h] = total
+    for i in range(3):
+        xx, yy = (x + OFFSETS[i]) % NX, (y + OFFSETS[i]) % NY
+        pending.append(
+            send(gb.at[0, yy], gb_recv.at[0, y], gb_ss.at[0, i], gb_rs.at[0, y], yy * NX + x, c)
+        )
+        pending.append(
+            send(gb.at[1, xx], gb_recv.at[1, x], gb_ss.at[1, i], gb_rs.at[1, x], y * NX + xx, c)
+        )
 
     for oy, ox, ok in PLANE_K:
         frm = plane(oy, ox) * NK + (k + ok) % NK
@@ -275,6 +316,32 @@
     products = dot(image_t, xcat[...], HIGHEST)
     inner = (inner2[0:RANK, :] + pltpu.roll(inner2[RANK:, :], RANK, 1)) * F32(1.0 / MODE)
     product = products[0:RANK, 0:LANES] + products[RANK:, LANES:]
+    halves = []
+    for h, at in ((0, y), (1, x)):
+        total = gb[h, at]
+        for i in range(3):
+            frm = (at + OFFSETS[i]) % 4
+            arrival(gb_recv.at[h, frm], gb_ss.at[h, 0], gb_rs.at[h, frm]).wait_recv()
+            total = total + gb_recv[h, frm]
+        halves.append(total)
+    total = jnp.concatenate(halves, axis=0)
+    low_width = 128 * (r // 4 + 1)
+    lane = lax.broadcasted_iota(jnp.int32, (2, GW), 1)
+    for t in range(8):
+        pair = jnp.where(lane < low_width, total[2 * t : 2 * t + 2], total[14 - 2 * t : 16 - 2 * t])
+        gz_send[t] = pair
+    for t in range(8):
+        zz, kk = 4 * k + t // 2, t % 2
+        mine = jnp.logical_and(zz == z, kk == k)
+
+        @pl.when(jnp.logical_not(mine))
+        def _():
+            send(gz_send.at[t], gz_recv.at[z], gz_ss.at[t], gz_rs.at[z], r, column(zz, kk))
+
+        @pl.when(mine)
+        def _():
+            gz_recv[z] = gz_send[t]
+
     inv_high = eliminate(inner)
     inv_low = pltpu.roll(inv_high, RANK, 1)
     core = dot(inv_low[:, 0:RANK], product, HIGHEST) * F32(1.0 / math.sqrt(MODE))
@@ -285,29 +352,6 @@
     c_recv[r] = c_send[r]
     nf_out[:, 0 : MODE // 2] = dot_t(inv_low, image, HIGHEST)
     nf_out[:, MODE // 2 :] = dot_t(inv_high, image, HIGHEST)
-
-    for oy, ox in PLANE:
-        frm = plane(oy, ox)
-        arrival(g_recv.at[frm], g_ss.at[0], g_rs.at[frm]).wait_recv()
-    total = g_recv[0]
-    for s in range(1, NR):
-        total = total + g_recv[s]
-    low_width = 128 * (r // 4 + 1)
-    lane = lax.broadcasted_iota(jnp.int32, (2, GW), 1)
-    for t in range(8):
-        pair = jnp.where(lane < low_width, total[2 * t : 2 * t + 2], total[14 - 2 * t : 16 - 2 * t])
-        gz_send[t] = pair
-    for t in range(8):
-        zz, kk = 4 * k + t // 2, t % 2
-        mine = jnp.logical_and(zz == z, kk == k)
-
-        @pl.when(jnp.logical_not(mine))
-        def _():
-            send(gz_send.at[t], gz_recv.at[z], gz_ss.at[t], gz_rs.at[z], r, column(zz, kk))
-
-        @pl.when(mine)
-        def _():
-            gz_recv[z] = gz_send[t]
 
     for oy, ox in PLANE:
         frm = plane(oy, ox)
@@ -370,8 +414,10 @@
             pltpu.VMEM((NR, RANK // NR, LANES), F32),
             pltpu.VMEM((MODE // 2, 6 * LANES), BF16),
             pltpu.VMEM((MODE, 6 * LANES), BF16),
-            pltpu.VMEM((NR, 16, GW), F32),
-            pltpu.VMEM((NR, 16, GW), F32),
+            pltpu.VMEM((2, 4, 4, 8, GW), F32),
+            pltpu.VMEM((2, 4, 4, 8, GW), F32),
+            pltpu.VMEM((2, 4, 8, GW), F32),
+            pltpu.VMEM((2, 4, 8, GW), F32),
             pltpu.VMEM((8, 2, GW), F32),
             pltpu.VMEM((NZ, 2, GW), F32),
             pltpu.VMEM((2, 1536), F32),
@@ -388,12 +434,16 @@
             dma((NR * NK,)),
             dma((NR - 1,)),
             dma((NR,)),
-            dma((NR - 1,)),
-            dma((NR,)),
+            dma((2, 3)),
+            dma((2, 4)),
+            dma((2, 3)),
+            dma((2, 4)),
             dma((8,)),
             dma((NZ,)),
         ],
-        compiler_params=pltpu.CompilerParams(collective_id=0, has_side_effects=True),
+        compiler_params=pltpu.CompilerParams(
+            collective_id=0, has_side_effects=True, vmem_limit_bytes=32 * 1024 * 1024
+        ),
         name="tucker_update",
     )(unfolding, factor.T)
     return gram_lower, new_factor_t.T, core

time: 68.1 us -> 53.4 us (0.78)
  Pallas kernels: 63.6 us -> 48.7 us
    pallas_call x1, Pallas kernels: 63.6 us -> 48.7 us  [body(): pl.pallas_call(kernel, out_shape=(jax.ShapeDtypeStruct((4, MODE), F32), j...]
    unnamed x5 -> x7, local copies, waits for them, and re-layouts: 3.62 us -> 3.91 us
where the time goes in v3:
time: 53.4 us; the launch traced here: 53.3 us
  Pallas kernels  48.7 us (91%)
  local copies, waits for them, and re-layouts  3.91 us (7%)
  between operations  0.65 us (1%)
    pallas_call x1, Pallas kernels, body(): pl.pallas_call(kernel, out_shape=(jax.ShapeDtypeStruct((4, MODE), F32), j...  48.7 us
    unnamed x7, local copies, waits for them, and re-layouts  3.91 us

profile of v3, /device:TPU:1, one launch (start us, length us, event | category | flops | bytes accessed | tf_op | source)
XLA Modules:
  0.0 53.3 jit_solution(11908258227602457313)
XLA Ops:
  0.6 0.0 copy-start
  0.6 1.0 %copy-done = f32[64,2048]{1,0:T(8,128)S(1)} copy-done((f32[64,2048]{1,0:T(8,128)S(1)}, f32[64,2048]{1,0:T(8,128)}, u32[]{:S(2)}) %copy-start) | copy-done | bytes 524312
  1.7 0.0 copy-start.1
  1.7 0.9 %copy-done.1 = f32[1024,64]{0,1:T(8,128)S(1)} copy-done((f32[1024,64]{0,1:T(8,128)S(1)}, f32[1024,64]{0,1:T(8,128)}, u32[]{:S(2)}) %copy-start.1) | copy-done | bytes 262168
  2.6 48.7 %tucker_update.1 = (f32[4,1024]{1,0:T(4,128)S(1)}, f32[64,1024]{1,0:T(8,128)S(1)}, f32[4,2048]{1,0:T(4,128)S(1)}) custom-call(f32[64,2048]{1,0:T(8,128)S(1)} %copy-done, f32[64,1024]{1,0:T(8,128)S(1)} %bitcast.2), custom_call_target="tpu_custom_call" | custom-call | tf_op jit(solution)/shard_map/tucker_update/pallas_call | solution.py:395
  51.3 0.6 %copy.8 = f32[4,1024]{1,0:T(4,128)} copy(f32[4,1024]{1,0:T(4,128)S(1)} %get-tuple-element.12) | data formatting | bytes 32768
  51.9 0.7 %copy.9 = f32[1024,64]{0,1:T(8,128)} copy(f32[1024,64]{0,1:T(8,128)S(1)} %bitcast.3) | data formatting | bytes 524288
  52.6 0.6 %copy.10 = f32[4,2048]{1,0:T(4,128)} copy(f32[4,2048]{1,0:T(4,128)S(1)} %get-tuple-element.14) | data formatting | bytes 65536
Async XLA Ops:
  0.6 1.0 %copy-start = (f32[64,2048]{1,0:T(8,128)S(1)}, f32[64,2048]{1,0:T(8,128)}, u32[]{:S(2)}) copy-start(f32[64,2048]{1,0:T(8,128)} %x_hbm.1) | copy-start | bytes 1572868
  1.7 0.9 %copy-start.1 = (f32[1024,64]{0,1:T(8,128)S(1)}, f32[1024,64]{0,1:T(8,128)}, u32[]{:S(2)}) copy-start(f32[1024,64]{0,1:T(8,128)} %param.3) | copy-start | bytes 786436

commit v4 on v3

--- a/solution.py
+++ b/solution.py
@@ -39,6 +39,21 @@
     return lax.dot_general(
         a, b, (((1,), (0,)), ((), ())), precision=precision, preferred_element_type=F32
     )
+
+
+def split(a):
+    hi = a.astype(BF16)
+    return hi, (a - hi.astype(F32)).astype(BF16)
+
+
+def dot3(a, b):
+    (ah, al), (bh, bl) = split(a), split(b)
+    return dot(jnp.concatenate([ah, ah, al], axis=1), jnp.concatenate([bh, bl, bh], axis=0))
+
+
+def dot3_t(a, b):
+    (ah, al), (bh, bl) = split(a), split(b)
+    return dot_t(jnp.concatenate([ah, ah, al], axis=1), jnp.concatenate([bh, bl, bh], axis=1))
 
 
 def eliminate(inner):
@@ -84,11 +99,12 @@
 
 def kernel(
     x_hbm,
-    ft,
+    ft_hbm,
     gram_out,
     nf_out,
     core_out,
     xr,
+    ft,
     xcat,
     img_send,
     img_recv,
@@ -108,6 +124,7 @@
     gz_recv,
     gfin,
     own_sem,
+    ft_sem,
     x_ss,
     x_rs,
     pair_ss,
@@ -162,14 +179,6 @@
 
     barrier = pltpu.get_barrier_semaphore()
     peers = 0
-    for oy, ox, ok in PLANE_K:
-        pl.semaphore_signal(
-            barrier,
-            inc=1,
-            device_id=(plane(oy, ox), column(z, (k + ok) % NK)),
-            device_id_type=MESH,
-        )
-        peers += 1
     for oz in ZS:
         for ok in range(NK):
             pl.semaphore_signal(
@@ -179,6 +188,16 @@
                 device_id_type=MESH,
             )
             peers += 1
+    for oy, ox, ok in PLANE_K:
+        pl.semaphore_signal(
+            barrier,
+            inc=1,
+            device_id=(plane(oy, ox), column(z, (k + ok) % NK)),
+            device_id_type=MESH,
+        )
+        peers += 1
+    factor_copy = pltpu.make_async_copy(ft_hbm, ft, ft_sem)
+    factor_copy.start()
     pl.semaphore_wait(barrier, peers)
 
     pending = []
@@ -194,6 +213,7 @@
     own = pltpu.make_async_copy(x_hbm.at[:, columns_of(r)], xr.at[0, r], own_sem)
     own.start()
     own.wait()
+    factor_copy.wait()
     for oy, ox in PLANE:
         frm = plane(oy, ox)
         arrival(xr.at[0, frm], x_ss.at[0], x_rs.at[frm]).wait_recv()
@@ -203,12 +223,12 @@
     flat = xr[0].reshape(MODE, LANES)
     xcat[:, 0:LANES] = flat[0 : MODE // 2]
     xcat[:, LANES : 2 * LANES] = flat[MODE // 2 :]
-    yt = dot(ft[...], flat, HIGHEST) * F32(1.0 / COLS)
+    yt = dot3(ft[...], flat) * F32(1.0 / COLS)
     zero = jnp.zeros_like(yt)
     weights = jnp.concatenate(
         [jnp.concatenate([yt, zero], axis=1), jnp.concatenate([zero, yt], axis=1)], axis=0
     )
-    term = dot_t(xcat[...], weights, HIGHEST)
+    term = dot3_t(xcat[...], weights)
     img_send[...] = term.reshape(NR, NK, 16, 128)
     me = r * NK + k
     for i, (oy, ox, ok) in enumerate(PLANE_K):
@@ -312,10 +332,21 @@
 
     image = p_all[...].reshape(MODE // 2, 128)
     image_t = image.T
-    inner2 = dot(image_t, image, HIGHEST)
-    products = dot(image_t, xcat[...], HIGHEST)
+    inner2 = dot3(image_t, image)
+    products = dot3(image_t, xcat[...])
     inner = (inner2[0:RANK, :] + pltpu.roll(inner2[RANK:, :], RANK, 1)) * F32(1.0 / MODE)
     product = products[0:RANK, 0:LANES] + products[RANK:, LANES:]
+    inv_high = eliminate(inner)
+    inv_low = pltpu.roll(inv_high, RANK, 1)
+    core = dot(inv_low[:, 0:RANK], product, HIGHEST) * F32(1.0 / math.sqrt(MODE))
+    c_send[...] = core.reshape(NR, RANK // NR, LANES)
+    for i, (oy, ox) in enumerate(PLANE):
+        to = plane(oy, ox)
+        pending.append(send(c_send.at[to], c_recv.at[r], c_ss.at[i], c_rs.at[r], to, c))
+    c_recv[r] = c_send[r]
+    nf_out[:, 0 : MODE // 2] = dot3_t(inv_low, image)
+    nf_out[:, MODE // 2 :] = dot3_t(inv_high, image)
+
     halves = []
     for h, at in ((0, y), (1, x)):
         total = gb[h, at]
@@ -342,17 +373,6 @@
         def _():
             gz_recv[z] = gz_send[t]
 
-    inv_high = eliminate(inner)
-    inv_low = pltpu.roll(inv_high, RANK, 1)
-    core = dot(inv_low[:, 0:RANK], product, HIGHEST) * F32(1.0 / math.sqrt(MODE))
-    c_send[...] = core.reshape(NR, RANK // NR, LANES)
-    for i, (oy, ox) in enumerate(PLANE):
-        to = plane(oy, ox)
-        pending.append(send(c_send.at[to], c_recv.at[r], c_ss.at[i], c_rs.at[r], to, c))
-    c_recv[r] = c_send[r]
-    nf_out[:, 0 : MODE // 2] = dot_t(inv_low, image, HIGHEST)
-    nf_out[:, MODE // 2 :] = dot_t(inv_high, image, HIGHEST)
-
     for oy, ox in PLANE:
         frm = plane(oy, ox)
         arrival(c_recv.at[frm], c_ss.at[0], c_rs.at[frm]).wait_recv()
@@ -389,8 +409,18 @@
             arrival(gz_send.at[t], gz_ss.at[t], gz_rs.at[0]).wait_send()
 
 
+def finish(gram_in, nf_in, core_in, gram_out, nf_out, core_out, sems):
+    copies = []
+    for i, (src, dst) in enumerate(((nf_in, nf_out), (core_in, core_out), (gram_in, gram_out))):
+        copies.append(pltpu.make_async_copy(src, dst, sems.at[i]))
+        copies[-1].start()
+    for copy in copies:
+        copy.wait()
+
+
 def body(unfolding, factor):
     dma = pltpu.SemaphoreType.DMA
+    hbm = functools.partial(pltpu.with_memory_space_constraint, memory_space=pltpu.HBM)
     vmem = pl.BlockSpec(memory_space=pltpu.VMEM)
     gram_lower, new_factor_t, core = pl.pallas_call(
         kernel,
@@ -399,10 +429,11 @@
             jax.ShapeDtypeStruct((RANK, MODE), F32),
             jax.ShapeDtypeStruct((RANK // NR, LANES * NR), F32),
         ),
-        in_specs=[pl.BlockSpec(memory_space=pl.ANY), vmem],
+        in_specs=[pl.BlockSpec(memory_space=pl.ANY)] * 2,
         out_specs=(vmem, vmem, vmem),
         scratch_shapes=[
             pltpu.VMEM((2, NR, ROWS, LANES), F32),
+            pltpu.VMEM((RANK, MODE), F32),
             pltpu.VMEM((MODE // 2, 2 * LANES), F32),
             pltpu.VMEM((NR, NK, 16, 128), F32),
             pltpu.VMEM((NR * NK, 16, 128), F32),
@@ -421,6 +452,7 @@
             pltpu.VMEM((8, 2, GW), F32),
             pltpu.VMEM((NZ, 2, GW), F32),
             pltpu.VMEM((2, 1536), F32),
+            dma,
             dma,
             dma((NR - 1,)),
             dma((NR,)),
@@ -445,7 +477,21 @@
             collective_id=0, has_side_effects=True, vmem_limit_bytes=32 * 1024 * 1024
         ),
         name="tucker_update",
-    )(unfolding, factor.T)
+    )(hbm(unfolding), hbm(factor.T))
+    anywhere = pl.BlockSpec(memory_space=pl.ANY)
+    gram_lower, new_factor_t, core = pl.pallas_call(
+        finish,
+        out_shape=(
+            jax.ShapeDtypeStruct((4, MODE), F32),
+            jax.ShapeDtypeStruct((RANK, MODE), F32),
+            jax.ShapeDtypeStruct((RANK // NR, LANES * NR), F32),
+        ),
+        in_specs=[anywhere, anywhere, anywhere],
+        out_specs=(anywhere, anywhere, anywhere),
+        scratch_shapes=[pltpu.SemaphoreType.DMA((3,))],
+        compiler_params=pltpu.CompilerParams(vmem_limit_bytes=1024 * 1024),
+        name="write_results",
+    )(gram_lower, new_factor_t, core)
     return gram_lower, new_factor_t.T, core
 
 

time: 53.4 us -> 49.3 us (0.923)
  local copies, waits for them, and re-layouts: 3.91 us -> 0 us
    unnamed x7 -> x0, local copies, waits for them, and re-layouts: 3.91 us -> none
    pallas_call x1, Pallas kernels: 48.7 us -> 47.8 us  [body(): pl.pallas_call(kernel, out_shape=(jax.ShapeDtypeStruct((4, MODE), F32), j...]
    pallas_call x0 -> x1, Pallas kernels: none -> 0.74 us  [body(): pl.pallas_call(finish, out_shape=(jax.ShapeDtypeStruct((4, MODE), F32), j...]
where the time goes in v4:
time: 49.3 us; the launch traced here: 49.1 us
  Pallas kernels  48.5 us (98%)
  between operations  0.64 us (1%)
    pallas_call x1, Pallas kernels, body(): pl.pallas_call(kernel, out_shape=(jax.ShapeDtypeStruct((4, MODE), F32), j...  47.8 us

profile of v4, /device:TPU:1, one launch (start us, length us, event | category | flops | bytes accessed | tf_op | source)
XLA Modules:
  0.0 49.1 jit_solution(6571550542904557823)
XLA Ops:
  0.6 47.8 %tucker_update.1 = (f32[4,1024]{1,0:T(4,128)S(1)}, f32[64,1024]{1,0:T(8,128)S(1)}, f32[4,2048]{1,0:T(4,128)S(1)}) custom-call(f32[64,2048]{1,0:T(8,128)} %x_hbm.1, f32[64,1024]{1,0:T(8,128)} %bitcast.2), custom_call_target="tpu_custom_call" | custom-call | tf_op jit(solution)/shard_map/tucker_update/pallas_call | solution.py:425
  48.4 0.7 %write_results.1 = (f32[4,1024]{1,0:T(4,128)}, f32[64,1024]{1,0:T(8,128)}, f32[4,2048]{1,0:T(4,128)}) custom-call(f32[4,1024]{1,0:T(4,128)S(1)} %get-tuple-element.9.gram_in, f32[64,1024]{1,0:T(8,128)S(1)} %get-tuple-element.10.nf_in, f32[4,2048]{1,0:T(4,128)S(1)} %get-tuple-element.11.core_in), custom_call_target="tpu_custom_call" | custom-call | tf_op jit(solution)/shard_map/write_results/pallas_call | solution.py:482

commit v5 on v4

--- a/solution.py
+++ b/solution.py
@@ -259,6 +259,13 @@
         lhs[16 * b : 16 * b + 16, 0:256] = rhs[at, 0:256]
         lhs[16 * b : 16 * b + 16, 256:512] = rhs[at, 0:256]
         lhs[16 * b : 16 * b + 16, 512:768] = rhs[at, 256:512]
+    at_row = lax.broadcasted_iota(jnp.int32, (256, 256), 0)
+    at_col = lax.broadcasted_iota(jnp.int32, (256, 256), 1)
+    mirrored = at_row - at_row % 16 + 14 - at_row % 16 + 2 * (at_row % 2)
+    order = jnp.where(at_col == mirrored, F32(1.0), F32(0.0)).astype(BF16)
+    lhs[256:512, 0:256] = dot(order, lhs[256:512, 0:256]).astype(BF16)
+    lhs[256:512, 256:512] = lhs[256:512, 0:256]
+    lhs[256:512, 512:768] = dot(order, lhs[256:512, 512:768]).astype(BF16)
     for nb in range(4):
         part = dot_t(lhs[128 * nb : 512, :], rhs[256 * nb : 256 * nb + 256, :]) * F32(1.0 / COLS)
         for b in range(8 * nb, 2 * NR):
@@ -316,15 +323,19 @@
             frm = (at + OFFSETS[i]) % 4
             arrival(ga_recv.at[h, frm], ga_ss.at[h, 0], ga_rs.at[h, frm]).wait_recv()
             total = total + ga_recv[h, frm]
-        gb[h] = total
-    for i in range(3):
-        xx, yy = (x + OFFSETS[i]) % NX, (y + OFFSETS[i]) % NY
-        pending.append(
-            send(gb.at[0, yy], gb_recv.at[0, y], gb_ss.at[0, i], gb_rs.at[0, y], yy * NX + x, c)
-        )
-        pending.append(
-            send(gb.at[1, xx], gb_recv.at[1, x], gb_ss.at[1, i], gb_rs.at[1, x], y * NX + xx, c)
-        )
+        for t in range(4):
+            gz_send[4 * h + t] = total[:, 2 * t : 2 * t + 2]
+    for t in range(8):
+        zz, kk = 4 * k + t // 2, t % 2
+        mine = jnp.logical_and(zz == z, kk == k)
+
+        @pl.when(jnp.logical_not(mine))
+        def _():
+            send(gz_send.at[t], gz_recv.at[z], gz_ss.at[t], gz_rs.at[z], r, column(zz, kk))
+
+        @pl.when(mine)
+        def _():
+            gz_recv[z] = gz_send[t]
 
     for oy, ox, ok in PLANE_K:
         frm = plane(oy, ox) * NK + (k + ok) % NK
@@ -347,31 +358,23 @@
     nf_out[:, 0 : MODE // 2] = dot3_t(inv_low, image)
     nf_out[:, MODE // 2 :] = dot3_t(inv_high, image)
 
-    halves = []
-    for h, at in ((0, y), (1, x)):
-        total = gb[h, at]
-        for i in range(3):
-            frm = (at + OFFSETS[i]) % 4
-            arrival(gb_recv.at[h, frm], gb_ss.at[h, 0], gb_rs.at[h, frm]).wait_recv()
-            total = total + gb_recv[h, frm]
-        halves.append(total)
-    total = jnp.concatenate(halves, axis=0)
-    low_width = 128 * (r // 4 + 1)
-    lane = lax.broadcasted_iota(jnp.int32, (2, GW), 1)
-    for t in range(8):
-        pair = jnp.where(lane < low_width, total[2 * t : 2 * t + 2], total[14 - 2 * t : 16 - 2 * t])
-        gz_send[t] = pair
-    for t in range(8):
-        zz, kk = 4 * k + t // 2, t % 2
-        mine = jnp.logical_and(zz == z, kk == k)
-
-        @pl.when(jnp.logical_not(mine))
+    from_core = z // 4
+    for s in range(NZ):
+
+        @pl.when(jnp.logical_not(jnp.logical_and(s == z, from_core == k)))
         def _():
-            send(gz_send.at[t], gz_recv.at[z], gz_ss.at[t], gz_rs.at[z], r, column(zz, kk))
-
-        @pl.when(mine)
-        def _():
-            gz_recv[z] = gz_send[t]
+            arrival(gz_recv.at[s], gz_ss.at[0], gz_rs.at[s]).wait_recv()
+
+    total = gz_recv[0]
+    for s in range(1, NZ):
+        total = total + gz_recv[s]
+    gb[...] = total
+    along_y = z % 4 < 2
+    at = jnp.where(along_y, y, x)
+    for i in range(3):
+        to = (at + OFFSETS[i]) % 4
+        row = jnp.where(along_y, to * NX + x, y * NX + to)
+        pending.append(send(gb.at[to], gb_recv.at[at], gb_ss.at[i], gb_rs.at[at], row, c))
 
     for oy, ox in PLANE:
         frm = plane(oy, ox)
@@ -379,16 +382,12 @@
     for s in range(NR):
         core_out[:, LANES * s : LANES * (s + 1)] = c_recv[s]
 
-    from_core = z // 4
-    for s in range(NZ):
-
-        @pl.when(jnp.logical_not(jnp.logical_and(s == z, from_core == k)))
-        def _():
-            arrival(gz_recv.at[s], gz_ss.at[0], gz_rs.at[s]).wait_recv()
-
-    total = gz_recv[0]
-    for s in range(1, NZ):
-        total = total + gz_recv[s]
+    total = gb[at]
+    for i in range(3):
+        frm = (at + OFFSETS[i]) % 4
+        arrival(gb_recv.at[frm], gb_ss.at[0], gb_rs.at[frm]).wait_recv()
+        total = total + gb_recv[frm]
+    low_width = 128 * (r // 4 + 1)
     gfin[...] = jnp.zeros_like(gfin)
     gfin[:, 0:GW] = total
     owner = r * (NZ * NK) + c
@@ -447,10 +446,10 @@
             pltpu.VMEM((MODE, 6 * LANES), BF16),
             pltpu.VMEM((2, 4, 4, 8, GW), F32),
             pltpu.VMEM((2, 4, 4, 8, GW), F32),
-            pltpu.VMEM((2, 4, 8, GW), F32),
-            pltpu.VMEM((2, 4, 8, GW), F32),
-            pltpu.VMEM((8, 2, GW), F32),
-            pltpu.VMEM((NZ, 2, GW), F32),
+            pltpu.VMEM((4, 2, GW), F32),
+            pltpu.VMEM((4, 2, GW), F32),
+            pltpu.VMEM((8, 4, 2, GW), F32),
+            pltpu.VMEM((NZ, 4, 2, GW), F32),
             pltpu.VMEM((2, 1536), F32),
             dma,
             dma,
@@ -468,8 +467,8 @@
             dma((NR,)),
             dma((2, 3)),
             dma((2, 4)),
-            dma((2, 3)),
-            dma((2, 4)),
+            dma((3,)),
+            dma((4,)),
             dma((8,)),
             dma((NZ,)),
         ],

time: 49.3 us -> 48.6 us (0.986)
  Pallas kernels: 48.5 us -> 47.8 us
    pallas_call x1, Pallas kernels: 47.8 us -> 47 us  [body(): pl.pallas_call(kernel, out_shape=(jax.ShapeDtypeStruct((4, MODE), F32), j...]
where the time goes in v5:
time: 48.6 us; the launch traced here: 48.4 us
  Pallas kernels  47.8 us (98%)
  between operations  0.64 us (1%)
    pallas_call x1, Pallas kernels, body(): pl.pallas_call(kernel, out_shape=(jax.ShapeDtypeStruct((4, MODE), F32), j...  47 us

profile of v5, /device:TPU:1, one launch (start us, length us, event | category | flops | bytes accessed | tf_op | source)
XLA Modules:
  0.0 48.4 jit_solution(13298212078233018444)
XLA Ops:
  0.6 47.0 %tucker_update.1 = (f32[4,1024]{1,0:T(4,128)S(1)}, f32[64,1024]{1,0:T(8,128)S(1)}, f32[4,2048]{1,0:T(4,128)S(1)}) custom-call(f32[64,2048]{1,0:T(8,128)} %x_hbm.1, f32[64,1024]{1,0:T(8,128)} %bitcast.2), custom_call_target="tpu_custom_call" | custom-call | tf_op jit(solution)/shard_map/tucker_update/pallas_call | solution.py:424
  47.7 0.7 %write_results.1 = (f32[4,1024]{1,0:T(4,128)}, f32[64,1024]{1,0:T(8,128)}, f32[4,2048]{1,0:T(4,128)}) custom-call(f32[4,1024]{1,0:T(4,128)S(1)} %get-tuple-element.9.gram_in, f32[64,1024]{1,0:T(8,128)S(1)} %get-tuple-element.10.nf_in, f32[4,2048]{1,0:T(4,128)S(1)} %get-tuple-element.11.core_in), custom_call_target="tpu_custom_call" | custom-call | tf_op jit(solution)/shard_map/write_results/pallas_call | solution.py:481

commit v6 on v5

--- a/solution.py
+++ b/solution.py
@@ -25,7 +25,7 @@
 PLANE_K = [(oy, ox, ok) for oy in range(NY) for ox in range(NX) for ok in range(NK)]
 PLANE_K = [o for o in PLANE_K if o != (0, 0, 0)]
 PLANE_K.sort(key=lambda o: -(min(o[0], NY - o[0]) + min(o[1], NX - o[1])))
-OFFSETS = (2, 1, 3)
+OFFSETS = (1, 3, 2)
 ZS = sorted(range(1, NZ), key=lambda o: -min(o, NZ - o))
 
 
@@ -305,7 +305,7 @@
         total = total + z_recv[s]
     p_send[...] = total
     p_all[me] = total
-    for i, (oy, ox, ok) in enumerate(PLANE_K):
+    for i, (oy, ox, ok) in enumerate(sorted(PLANE_K, key=lambda o: min(o[0], NY - o[0]) + min(o[1], NX - o[1]))):
         pending.append(
             send(
                 p_send,
@@ -355,8 +355,6 @@
         to = plane(oy, ox)
         pending.append(send(c_send.at[to], c_recv.at[r], c_ss.at[i], c_rs.at[r], to, c))
     c_recv[r] = c_send[r]
-    nf_out[:, 0 : MODE // 2] = dot3_t(inv_low, image)
-    nf_out[:, MODE // 2 :] = dot3_t(inv_high, image)
 
     from_core = z // 4
     for s in range(NZ):
@@ -376,6 +374,8 @@
         row = jnp.where(along_y, to * NX + x, y * NX + to)
         pending.append(send(gb.at[to], gb_recv.at[at], gb_ss.at[i], gb_rs.at[at], row, c))
 
+    nf_out[:, 0 : MODE // 2] = dot3_t(inv_low, image)
+    nf_out[:, MODE // 2 :] = dot3_t(inv_high, image)
     for oy, ox in PLANE:
         frm = plane(oy, ox)
         arrival(c_recv.at[frm], c_ss.at[0], c_rs.at[frm]).wait_recv()

time: 48.6 us -> 47.1 us (0.969)
  Pallas kernels: 47.8 us -> 46.2 us
    pallas_call x1, Pallas kernels: 47 us -> 45.4 us  [body(): pl.pallas_call(kernel, out_shape=(jax.ShapeDtypeStruct((4, MODE), F32), j...]
where the time goes in v6:
time: 47.1 us; the launch traced here: 46.8 us
  Pallas kernels  46.2 us (98%)
  between operations  0.64 us (1%)
    pallas_call x1, Pallas kernels, body(): pl.pallas_call(kernel, out_shape=(jax.ShapeDtypeStruct((4, MODE), F32), j...  45.4 us

profile of v6, /device:TPU:1, one launch (start us, length us, event | category | flops | bytes accessed | tf_op | source)
XLA Modules:
  0.0 46.8 jit_solution(18241770059398413982)
XLA Ops:
  0.6 45.4 %tucker_update.1 = (f32[4,1024]{1,0:T(4,128)S(1)}, f32[64,1024]{1,0:T(8,128)S(1)}, f32[4,2048]{1,0:T(4,128)S(1)}) custom-call(f32[64,2048]{1,0:T(8,128)} %x_hbm.1, f32[64,1024]{1,0:T(8,128)} %bitcast.2), custom_call_target="tpu_custom_call" | custom-call | tf_op jit(solution)/shard_map/tucker_update/pallas_call | solution.py:424
  46.1 0.7 %write_results.1 = (f32[4,1024]{1,0:T(4,128)}, f32[64,1024]{1,0:T(8,128)}, f32[4,2048]{1,0:T(4,128)}) custom-call(f32[4,1024]{1,0:T(4,128)S(1)} %get-tuple-element.9.gram_in, f32[64,1024]{1,0:T(8,128)S(1)} %get-tuple-element.10.nf_in, f32[4,2048]{1,0:T(4,128)S(1)} %get-tuple-element.11.core_in), custom_call_target="tpu_custom_call" | custom-call | tf_op jit(solution)/shard_map/write_results/pallas_call | solution.py:481

commit v7 on v6

--- a/solution.py
+++ b/solution.py
@@ -179,6 +179,14 @@
 
     barrier = pltpu.get_barrier_semaphore()
     peers = 0
+    for oy, ox, ok in PLANE_K:
+        pl.semaphore_signal(
+            barrier,
+            inc=1,
+            device_id=(plane(oy, ox), column(z, (k + ok) % NK)),
+            device_id_type=MESH,
+        )
+        peers += 1
     for oz in ZS:
         for ok in range(NK):
             pl.semaphore_signal(
@@ -188,14 +196,6 @@
                 device_id_type=MESH,
             )
             peers += 1
-    for oy, ox, ok in PLANE_K:
-        pl.semaphore_signal(
-            barrier,
-            inc=1,
-            device_id=(plane(oy, ox), column(z, (k + ok) % NK)),
-            device_id_type=MESH,
-        )
-        peers += 1
     factor_copy = pltpu.make_async_copy(ft_hbm, ft, ft_sem)
     factor_copy.start()
     pl.semaphore_wait(barrier, peers)
@@ -205,18 +205,14 @@
     def columns_of(row):
         return pl.ds(pl.multiple_of(row * LANES, LANES), LANES)
 
-    for i, (oy, ox) in enumerate(PLANE):
+    for oy, ox in PLANE:
         to = plane(oy, ox)
-        pending.append(
-            send(x_hbm.at[:, columns_of(to)], xr.at[0, r], x_ss.at[i], x_rs.at[r], to, c)
-        )
+        send(x_hbm.at[:, columns_of(to)], xr.at[0, r], x_ss, x_rs, to, c)
     own = pltpu.make_async_copy(x_hbm.at[:, columns_of(r)], xr.at[0, r], own_sem)
     own.start()
     own.wait()
     factor_copy.wait()
-    for oy, ox in PLANE:
-        frm = plane(oy, ox)
-        arrival(xr.at[0, frm], x_ss.at[0], x_rs.at[frm]).wait_recv()
+    arrival(xr.at[0, 0 : NR - 1], x_ss, x_rs).wait_recv()
     partner = column(z, 1 - k)
     pending.append(send(xr.at[0], xr.at[1], pair_ss, pair_rs, r, partner))
 
@@ -231,18 +227,9 @@
     term = dot3_t(xcat[...], weights)
     img_send[...] = term.reshape(NR, NK, 16, 128)
     me = r * NK + k
-    for i, (oy, ox, ok) in enumerate(PLANE_K):
+    for oy, ox, ok in PLANE_K:
         to, kk = plane(oy, ox), (k + ok) % NK
-        pending.append(
-            send(
-                img_send.at[to, kk],
-                img_recv.at[me],
-                img_ss.at[i],
-                img_rs.at[me],
-                to,
-                column(z, kk),
-            )
-        )
+        send(img_send.at[to, kk], img_recv.at[me], img_ss, img_rs, to, column(z, kk))
     img_recv[me] = img_send[r, k]
 
     arrival(xr.at[1], pair_ss, pair_rs).wait_recv()
@@ -285,37 +272,22 @@
             send(ga.at[1, yy], ga_recv.at[1, y], ga_ss.at[1, i], ga_rs.at[1, y], yy * NX + x, c)
         )
 
-    for oy, ox, ok in PLANE_K:
-        frm = plane(oy, ox) * NK + (k + ok) % NK
-        arrival(img_recv.at[frm], img_ss.at[0], img_rs.at[frm]).wait_recv()
+    arrival(img_recv.at[0 : NR * NK - 1], img_ss, img_rs).wait_recv()
     total = img_recv[0]
     for s in range(1, NR * NK):
         total = total + img_recv[s]
     z_send[...] = total
     z_recv[z] = total
-    for i, oz in enumerate(ZS):
-        pending.append(
-            send(z_send, z_recv.at[z], z_ss.at[i], z_rs.at[z], r, column((z + oz) % NZ, k))
-        )
     for oz in ZS:
-        frm = (z + oz) % NZ
-        arrival(z_recv.at[frm], z_ss.at[0], z_rs.at[frm]).wait_recv()
+        send(z_send, z_recv.at[z], z_ss, z_rs, r, column((z + oz) % NZ, k))
+    arrival(z_recv.at[0 : NZ - 1], z_ss, z_rs).wait_recv()
     total = z_recv[0]
     for s in range(1, NZ):
         total = total + z_recv[s]
     p_send[...] = total
     p_all[me] = total
-    for i, (oy, ox, ok) in enumerate(sorted(PLANE_K, key=lambda o: min(o[0], NY - o[0]) + min(o[1], NX - o[1]))):
-        pending.append(
-            send(
-                p_send,
-                p_all.at[me],
-                p_ss.at[i],
-                p_rs.at[me],
-                plane(oy, ox),
-                column(z, (k + ok) % NK),
-            )
-        )
+    for oy, ox, ok in PLANE_K[::-1]:
+        send(p_send, p_all.at[me], p_ss, p_rs, plane(oy, ox), column(z, (k + ok) % NK))
 
     for h, at in ((0, x), (1, y)):
         total = ga[h, at]
@@ -337,9 +309,7 @@
         def _():
             gz_recv[z] = gz_send[t]
 
-    for oy, ox, ok in PLANE_K:
-        frm = plane(oy, ox) * NK + (k + ok) % NK
-        arrival(p_all.at[frm], p_ss.at[0], p_rs.at[frm]).wait_recv()
+    arrival(p_all.at[0 : NR * NK - 1], p_ss, p_rs).wait_recv()
 
     image = p_all[...].reshape(MODE // 2, 128)
     image_t = image.T
@@ -351,9 +321,9 @@
     inv_low = pltpu.roll(inv_high, RANK, 1)
     core = dot(inv_low[:, 0:RANK], product, HIGHEST) * F32(1.0 / math.sqrt(MODE))
     c_send[...] = core.reshape(NR, RANK // NR, LANES)
-    for i, (oy, ox) in enumerate(PLANE):
+    for oy, ox in PLANE:
         to = plane(oy, ox)
-        pending.append(send(c_send.at[to], c_recv.at[r], c_ss.at[i], c_rs.at[r], to, c))
+        send(c_send.at[to], c_recv.at[r], c_ss, c_rs, to, c)
     c_recv[r] = c_send[r]
 
     from_core = z // 4
@@ -376,9 +346,7 @@
 
     nf_out[:, 0 : MODE // 2] = dot3_t(inv_low, image)
     nf_out[:, MODE // 2 :] = dot3_t(inv_high, image)
-    for oy, ox in PLANE:
-        frm = plane(oy, ox)
-        arrival(c_recv.at[frm], c_ss.at[0], c_rs.at[frm]).wait_recv()
+    arrival(c_recv.at[0 : NR - 1], c_ss, c_rs).wait_recv()
     for s in range(NR):
         core_out[:, LANES * s : LANES * (s + 1)] = c_recv[s]
 
@@ -400,6 +368,11 @@
 
     for copy in pending:
         copy.wait_send()
+    arrival(xr.at[0, 0 : NR - 1], x_ss, x_rs).wait_send()
+    arrival(img_recv.at[0 : NR * NK - 1], img_ss, img_rs).wait_send()
+    arrival(z_recv.at[0 : NZ - 1], z_ss, z_rs).wait_send()
+    arrival(p_all.at[0 : NR * NK - 1], p_ss, p_rs).wait_send()
+    arrival(c_recv.at[0 : NR - 1], c_ss, c_rs).wait_send()
     for t in range(8):
         zz, kk = 4 * k + t // 2, t % 2
 
@@ -453,18 +426,18 @@
             pltpu.VMEM((2, 1536), F32),
             dma,
             dma,
-            dma((NR - 1,)),
-            dma((NR,)),
-            dma,
-            dma,
-            dma((NR * NK - 1,)),
-            dma((NR * NK,)),
-            dma((NZ - 1,)),
-            dma((NZ,)),
-            dma((NR * NK - 1,)),
-            dma((NR * NK,)),
-            dma((NR - 1,)),
-            dma((NR,)),
+            dma,
+            dma,
+            dma,
+            dma,
+            dma,
+            dma,
+            dma,
+            dma,
+            dma,
+            dma,
+            dma,
+            dma,
             dma((2, 3)),
             dma((2, 4)),
             dma((3,)),

time: 47.1 us -> 44.9 us (0.953)
  Pallas kernels: 46.2 us -> 44 us
    pallas_call x1, Pallas kernels: 45.4 us -> 43.3 us  [body(): pl.pallas_call(kernel, out_shape=(jax.ShapeDtypeStruct((4, MODE), F32), j...]
where the time goes in v7:
time: 44.9 us; the launch traced here: 44.7 us
  Pallas kernels  44 us (98%)
  between operations  0.64 us (1%)
    pallas_call x1, Pallas kernels, body(): pl.pallas_call(kernel, out_shape=(jax.ShapeDtypeStruct((4, MODE), F32), j...  43.3 us

profile of v7, /device:TPU:1, one launch (start us, length us, event | category | flops | bytes accessed | tf_op | source)
XLA Modules:
  0.0 44.7 jit_solution(3469583838741088104)
XLA Ops:
  0.6 43.3 %tucker_update.1 = (f32[4,1024]{1,0:T(4,128)S(1)}, f32[64,1024]{1,0:T(8,128)S(1)}, f32[4,2048]{1,0:T(4,128)S(1)}) custom-call(f32[64,2048]{1,0:T(8,128)} %x_hbm.1, f32[64,1024]{1,0:T(8,128)} %bitcast.2), custom_call_target="tpu_custom_call" | custom-call | tf_op jit(solution)/shard_map/tucker_update/pallas_call | solution.py:397
  43.9 0.7 %write_results.1 = (f32[4,1024]{1,0:T(4,128)}, f32[64,1024]{1,0:T(8,128)}, f32[4,2048]{1,0:T(4,128)}) custom-call(f32[4,1024]{1,0:T(4,128)S(1)} %get-tuple-element.9.gram_in, f32[64,1024]{1,0:T(8,128)S(1)} %get-tuple-element.10.nf_in, f32[4,2048]{1,0:T(4,128)S(1)} %get-tuple-element.11.core_in), custom_call_target="tpu_custom_call" | custom-call | tf_op jit(solution)/shard_map/write_results/pallas_call | solution.py:454

commit v8 on v7

--- a/solution.py
+++ b/solution.py
@@ -224,12 +224,19 @@
     weights = jnp.concatenate(
         [jnp.concatenate([yt, zero], axis=1), jnp.concatenate([zero, yt], axis=1)], axis=0
     )
-    term = dot3_t(xcat[...], weights)
-    img_send[...] = term.reshape(NR, NK, 16, 128)
     me = r * NK + k
-    for oy, ox, ok in PLANE_K:
-        to, kk = plane(oy, ox), (k + ok) % NK
-        send(img_send.at[to, kk], img_recv.at[me], img_ss, img_rs, to, column(z, kk))
+    wh, wl = split(weights)
+    wcat = jnp.concatenate([wh, wl, wh], axis=1)
+    for group in ((2, 1), (3, 0)):
+        for oy in group:
+            yy = (y + oy) % NY
+            ah, al = split(xcat[pl.ds(pl.multiple_of(yy * 128, 128), 128), :])
+            term = dot_t(jnp.concatenate([ah, ah, al], axis=1), wcat)
+            img_send[pl.ds(yy * NX, NX)] = term.reshape(NX, NK, 16, 128)
+        for oy, ox, ok in PLANE_K:
+            if oy in group:
+                to, kk = plane(oy, ox), (k + ok) % NK
+                send(img_send.at[to, kk], img_recv.at[me], img_ss, img_rs, to, column(z, kk))
     img_recv[me] = img_send[r, k]
 
     arrival(xr.at[1], pair_ss, pair_rs).wait_recv()
@@ -265,12 +272,8 @@
             ga[1, to // NX, to % NX, :, at] = rows_b[8:16]
     for i in range(3):
         xx, yy = (x + OFFSETS[i]) % NX, (y + OFFSETS[i]) % NY
-        pending.append(
-            send(ga.at[0, xx], ga_recv.at[0, x], ga_ss.at[0, i], ga_rs.at[0, x], y * NX + xx, c)
-        )
-        pending.append(
-            send(ga.at[1, yy], ga_recv.at[1, y], ga_ss.at[1, i], ga_rs.at[1, y], yy * NX + x, c)
-        )
+        send(ga.at[0, xx], ga_recv.at[0, x], ga_ss.at[0], ga_rs.at[0], y * NX + xx, c)
+        send(ga.at[1, yy], ga_recv.at[1, y], ga_ss.at[1], ga_rs.at[1], yy * NX + x, c)
 
     arrival(img_recv.at[0 : NR * NK - 1], img_ss, img_rs).wait_recv()
     total = img_recv[0]
@@ -290,11 +293,10 @@
         send(p_send, p_all.at[me], p_ss, p_rs, plane(oy, ox), column(z, (k + ok) % NK))
 
     for h, at in ((0, x), (1, y)):
+        arrival(ga_recv.at[h, 0:3], ga_ss.at[h], ga_rs.at[h]).wait_recv()
         total = ga[h, at]
         for i in range(3):
-            frm = (at + OFFSETS[i]) % 4
-            arrival(ga_recv.at[h, frm], ga_ss.at[h, 0], ga_rs.at[h, frm]).wait_recv()
-            total = total + ga_recv[h, frm]
+            total = total + ga_recv[h, (at + OFFSETS[i]) % 4]
         for t in range(4):
             gz_send[4 * h + t] = total[:, 2 * t : 2 * t + 2]
     for t in range(8):
@@ -303,7 +305,7 @@
 
         @pl.when(jnp.logical_not(mine))
         def _():
-            send(gz_send.at[t], gz_recv.at[z], gz_ss.at[t], gz_rs.at[z], r, column(zz, kk))
+            send(gz_send.at[t], gz_recv.at[z], gz_ss, gz_rs, r, column(zz, kk))
 
         @pl.when(mine)
         def _():
@@ -327,11 +329,14 @@
     c_recv[r] = c_send[r]
 
     from_core = z // 4
-    for s in range(NZ):
-
-        @pl.when(jnp.logical_not(jnp.logical_and(s == z, from_core == k)))
-        def _():
-            arrival(gz_recv.at[s], gz_ss.at[0], gz_rs.at[s]).wait_recv()
+
+    @pl.when(from_core == k)
+    def _():
+        arrival(gz_recv.at[0 : NZ - 1], gz_ss, gz_rs).wait_recv()
+
+    @pl.when(from_core != k)
+    def _():
+        arrival(gz_recv, gz_ss, gz_rs).wait_recv()
 
     total = gz_recv[0]
     for s in range(1, NZ):
@@ -342,7 +347,7 @@
     for i in range(3):
         to = (at + OFFSETS[i]) % 4
         row = jnp.where(along_y, to * NX + x, y * NX + to)
-        pending.append(send(gb.at[to], gb_recv.at[at], gb_ss.at[i], gb_rs.at[at], row, c))
+        send(gb.at[to], gb_recv.at[at], gb_ss, gb_rs, row, c)
 
     nf_out[:, 0 : MODE // 2] = dot3_t(inv_low, image)
     nf_out[:, MODE // 2 :] = dot3_t(inv_high, image)
@@ -350,11 +355,10 @@
     for s in range(NR):
         core_out[:, LANES * s : LANES * (s + 1)] = c_recv[s]
 
+    arrival(gb_recv.at[0:3], gb_ss, gb_rs).wait_recv()
     total = gb[at]
     for i in range(3):
-        frm = (at + OFFSETS[i]) % 4
-        arrival(gb_recv.at[frm], gb_ss.at[0], gb_rs.at[frm]).wait_recv()
-        total = total + gb_recv[frm]
+        total = total + gb_recv[(at + OFFSETS[i]) % 4]
     low_width = 128 * (r // 4 + 1)
     gfin[...] = jnp.zeros_like(gfin)
     gfin[:, 0:GW] = total
@@ -373,12 +377,17 @@
     arrival(z_recv.at[0 : NZ - 1], z_ss, z_rs).wait_send()
     arrival(p_all.at[0 : NR * NK - 1], p_ss, p_rs).wait_send()
     arrival(c_recv.at[0 : NR - 1], c_ss, c_rs).wait_send()
-    for t in range(8):
-        zz, kk = 4 * k + t // 2, t % 2
-
-        @pl.when(jnp.logical_not(jnp.logical_and(zz == z, kk == k)))
-        def _():
-            arrival(gz_send.at[t], gz_ss.at[t], gz_rs.at[0]).wait_send()
+    arrival(ga_recv.at[0, 0:3], ga_ss.at[0], ga_rs.at[0]).wait_send()
+    arrival(ga_recv.at[1, 0:3], ga_ss.at[1], ga_rs.at[1]).wait_send()
+    arrival(gb_recv.at[0:3], gb_ss, gb_rs).wait_send()
+
+    @pl.when(from_core == k)
+    def _():
+        arrival(gz_recv.at[0 : NZ - 1], gz_ss, gz_rs).wait_send()
+
+    @pl.when(from_core != k)
+    def _():
+        arrival(gz_recv, gz_ss, gz_rs).wait_send()
 
 
 def finish(gram_in, nf_in, core_in, gram_out, nf_out, core_out, sems):
@@ -438,12 +447,12 @@
             dma,
             dma,
             dma,
-            dma((2, 3)),
-            dma((2, 4)),
-            dma((3,)),
-            dma((4,)),
-            dma((8,)),
-            dma((NZ,)),
+            dma((2,)),
+            dma((2,)),
+            dma,
+            dma,
+            dma,
+            dma,
         ],
         compiler_params=pltpu.CompilerParams(
             collective_id=0, has_side_effects=True, vmem_limit_bytes=32 * 1024 * 1024

time: 44.9 us -> 44.5 us (level)
  no operation moved by 1% of the time
where the time goes in v8:
time: 44.5 us; the launch traced here: 44.3 us
  Pallas kernels  43.7 us (98%)
  between operations  0.64 us (1%)
    pallas_call x1, Pallas kernels, body(): pl.pallas_call(kernel, out_shape=(jax.ShapeDtypeStruct((4, MODE), F32), j...  43 us

profile of v8, /device:TPU:1, one launch (start us, length us, event | category | flops | bytes accessed | tf_op | source)
XLA Modules:
  0.0 44.3 jit_solution(5307040452315492351)
XLA Ops:
  0.6 43.0 %tucker_update.1 = (f32[4,1024]{1,0:T(4,128)S(1)}, f32[64,1024]{1,0:T(8,128)S(1)}, f32[4,2048]{1,0:T(4,128)S(1)}) custom-call(f32[64,2048]{1,0:T(8,128)} %x_hbm.1, f32[64,1024]{1,0:T(8,128)} %bitcast.2), custom_call_target="tpu_custom_call" | custom-call | tf_op jit(solution)/shard_map/tucker_update/pallas_call | solution.py:406
  43.6 0.7 %write_results.1 = (f32[4,1024]{1,0:T(4,128)}, f32[64,1024]{1,0:T(8,128)}, f32[4,2048]{1,0:T(4,128)}) custom-call(f32[4,1024]{1,0:T(4,128)S(1)} %get-tuple-element.9.gram_in, f32[64,1024]{1,0:T(8,128)S(1)} %get-tuple-element.10.nf_in, f32[4,2048]{1,0:T(4,128)S(1)} %get-tuple-element.11.core_in), custom_call_target="tpu_custom_call" | custom-call | tf_op jit(solution)/shard_map/write_results/pallas_call | solution.py:463

commit v9 on v8

--- a/solution.py
+++ b/solution.py
@@ -351,10 +351,6 @@
 
     nf_out[:, 0 : MODE // 2] = dot3_t(inv_low, image)
     nf_out[:, MODE // 2 :] = dot3_t(inv_high, image)
-    arrival(c_recv.at[0 : NR - 1], c_ss, c_rs).wait_recv()
-    for s in range(NR):
-        core_out[:, LANES * s : LANES * (s + 1)] = c_recv[s]
-
     arrival(gb_recv.at[0:3], gb_ss, gb_rs).wait_recv()
     total = gb[at]
     for i in range(3):
@@ -369,6 +365,10 @@
     high = gfin[:, pl.ds(pl.multiple_of(low_width, 128), MODE)]
     gram_out[0:2, :] = jnp.where(col_id <= 2 * owner + row_id, low, 0.0)
     gram_out[2:4, :] = jnp.where(col_id <= MODE - 2 - 2 * owner + row_id, high, 0.0)
+
+    arrival(c_recv.at[0 : NR - 1], c_ss, c_rs).wait_recv()
+    for s in range(NR):
+        core_out[:, LANES * s : LANES * (s + 1)] = c_recv[s]
 
     for copy in pending:
         copy.wait_send()

time: 44.5 us -> 44.5 us (level)
  no operation moved by 1% of the time
where the time goes in v9:
time: 44.5 us; the launch traced here: 44.4 us
  Pallas kernels  43.7 us (98%)
  between operations  0.64 us (1%)
    pallas_call x1, Pallas kernels, body(): pl.pallas_call(kernel, out_shape=(jax.ShapeDtypeStruct((4, MODE), F32), j...  43 us

profile of v9, /device:TPU:1, one launch (start us, length us, event | category | flops | bytes accessed | tf_op | source)
XLA Modules:
  0.0 44.4 jit_solution(13573115344390168586)
XLA Ops:
  0.6 43.0 %tucker_update.1 = (f32[4,1024]{1,0:T(4,128)S(1)}, f32[64,1024]{1,0:T(8,128)S(1)}, f32[4,2048]{1,0:T(4,128)S(1)}) custom-call(f32[64,2048]{1,0:T(8,128)} %x_hbm.1, f32[64,1024]{1,0:T(8,128)} %bitcast.2), custom_call_target="tpu_custom_call" | custom-call | tf_op jit(solution)/shard_map/tucker_update/pallas_call | solution.py:406
  43.6 0.7 %write_results.1 = (f32[4,1024]{1,0:T(4,128)}, f32[64,1024]{1,0:T(8,128)}, f32[4,2048]{1,0:T(4,128)}) custom-call(f32[4,1024]{1,0:T(4,128)S(1)} %get-tuple-element.9.gram_in, f32[64,1024]{1,0:T(8,128)S(1)} %get-tuple-element.10.nf_in, f32[4,2048]{1,0:T(4,128)S(1)} %get-tuple-element.11.core_in), custom_call_target="tpu_custom_call" | custom-call | tf_op jit(solution)/shard_map/write_results/pallas_call | solution.py:463

commit v10 on v9

--- a/solution.py
+++ b/solution.py
@@ -321,7 +321,7 @@
     product = products[0:RANK, 0:LANES] + products[RANK:, LANES:]
     inv_high = eliminate(inner)
     inv_low = pltpu.roll(inv_high, RANK, 1)
-    core = dot(inv_low[:, 0:RANK], product, HIGHEST) * F32(1.0 / math.sqrt(MODE))
+    core = dot3(inv_low[:, 0:RANK], product) * F32(1.0 / math.sqrt(MODE))
     c_send[...] = core.reshape(NR, RANK // NR, LANES)
     for oy, ox in PLANE:
         to = plane(oy, ox)

time: 44.5 us -> 44.5 us (level)
  no operation moved by 1% of the time
where the time goes in v10:
time: 44.5 us; the launch traced here: 44.3 us
  Pallas kernels  43.7 us (98%)
  between operations  0.64 us (1%)
    pallas_call x1, Pallas kernels, body(): pl.pallas_call(kernel, out_shape=(jax.ShapeDtypeStruct((4, MODE), F32), j...  42.9 us

profile of v10, /device:TPU:1, one launch (start us, length us, event | category | flops | bytes accessed | tf_op | source)
XLA Modules:
  0.0 44.3 jit_solution(2538931958025442626)
XLA Ops:
  0.6 42.9 %tucker_update.1 = (f32[4,1024]{1,0:T(4,128)S(1)}, f32[64,1024]{1,0:T(8,128)S(1)}, f32[4,2048]{1,0:T(4,128)S(1)}) custom-call(f32[64,2048]{1,0:T(8,128)} %x_hbm.1, f32[64,1024]{1,0:T(8,128)} %bitcast.2), custom_call_target="tpu_custom_call" | custom-call | tf_op jit(solution)/shard_map/tucker_update/pallas_call | solution.py:406
  43.6 0.7 %write_results.1 = (f32[4,1024]{1,0:T(4,128)}, f32[64,1024]{1,0:T(8,128)}, f32[4,2048]{1,0:T(4,128)}) custom-call(f32[4,1024]{1,0:T(4,128)S(1)} %get-tuple-element.9.gram_in, f32[64,1024]{1,0:T(8,128)S(1)} %get-tuple-element.10.nf_in, f32[4,2048]{1,0:T(4,128)S(1)} %get-tuple-element.11.core_in), custom_call_target="tpu_custom_call" | custom-call | tf_op jit(solution)/shard_map/write_results/pallas_call | solution.py:463
